TPU v7x, 128 devices: a whole 4x4x4 slice. The times are simulated.
128 devices in a mesh: store: 32 (over z, x, core), tensor: 4 (over y).
Axes of the slice: x: 4, y: 4, z: 4, core: 2. Of those that a mesh axis runs over, the one named last changes fastest.
Arguments:
- eval_inputs: bfloat16 [24576, 4096], P('store'), may hold values from -6 to 6
- eval_grads: bfloat16 [24576, 4096], P('store'), may hold values from -6 to 6
- w_gate: bfloat16 [4096, 7168], P('store', 'tensor'), may hold values from -0.09375 to 0.09375
- w_down: bfloat16 [7168, 4096], P('tensor', 'store'), may hold values from -0.0625 to 0.0625
- proj_in: bfloat16 [4096, 64], replicated, may hold values from -0.09375 to 0.09375
- proj_out: bfloat16 [7168, 64], P('tensor'), may hold values from -0.0625 to 0.0625
- store_rows: bfloat16 [131072, 4096], P('store', 'tensor'), may hold values from -3 to 3
- eval_strata: int32 [192], replicated, may hold values from 0 to 7, as said below
- block_strata: int32 [1024], P('store'), may hold values from 0 to 7
Outputs:
- scores: float32 [192, 131072], P('tensor', 'store')
Inputs may be any that keep to these rules, and one draw needn't show every extreme that they name: `eval_strata`: each of the 8 strata is named by exactly 24 evaluation sequences.
All inputs are finite; a program needn't handle non-finite values.
Results may differ from a plain program's by a relative error of at most 0.0041.
Values may be sent and summed in bfloat16 or wider, within the bound.
A program may use at most 192 MiB of HBM per device.

v0:
```python
import jax
import jax.numpy as jnp
from jax import lax
from jax.sharding import PartitionSpec as P

RANK = 64
SEQ_LEN = 128
BLOCK = 128
STRATA = 8


def sent_together(arrays, axis, dim, along):
    widths = [a.shape[along] for a in arrays]
    both = jnp.concatenate(arrays, axis=along)
    filled = lax.all_gather(both, axis, axis=dim, tiled=True)
    return tuple(jnp.split(filled, [sum(widths[:k]) for k in range(1, len(widths))], axis=along))


def cut_along(x, dim, length):
    before, after = (x.shape[:dim], x.shape[dim + 1 :])
    return jnp.moveaxis(x.reshape(*before, length, -1, *after), dim, 0)


def sent_and_summed(x, axis, dim):
    length = lax.axis_size(axis)
    parts = lax.all_to_all(cut_along(x, dim, length), axis, 0, 0, tiled=True)
    return jnp.sum(parts, axis=0)


def from_everyone(x, axis):
    length = lax.axis_size(axis)
    return lax.all_to_all(jnp.broadcast_to(x[None], (length, *x.shape)), axis, 0, 0, tiled=True)


def laid_out(parts, dim):
    dims = list(parts.shape[1:])
    dims[dim] *= parts.shape[0]
    return jnp.moveaxis(parts, 0, dim).reshape(dims)


def gather_directly(x, axis, dim):
    parts = from_everyone(x, axis)
    return laid_out(parts, dim)


def taken_together(x, axis):
    everything = from_everyone(x, axis)
    return jnp.sum(everything, axis=0)


def add_columns(source, block_piece):
    return jnp.dot(source, block_piece, preferred_element_type=jnp.float32)


def outer_mean(left_proj, right_proj, seq_count):
    left_seq = left_proj.reshape(seq_count, SEQ_LEN, left_proj.shape[1])
    right_seq = right_proj.reshape(seq_count, SEQ_LEN, right_proj.shape[1])
    return (
        jnp.einsum("sti,stj->sij", left_seq, right_seq, precision=lax.Precision.HIGHEST) / SEQ_LEN
    )


def stratum_rank(eval_strata):
    onehot = (eval_strata[:, None] == jnp.arange(STRATA, dtype=jnp.int32)[None, :]).astype(
        jnp.int32
    )
    earlier = jnp.cumsum(onehot, axis=0) - onehot
    return jnp.sum(earlier * onehot, axis=1)


def stratum_blocks(gathered, eval_strata, block_strata, store_rows):
    total_eval = gathered.shape[0]
    feature_cols = store_rows.shape[1]
    per_stratum = total_eval // STRATA
    within = stratum_rank(eval_strata)
    slot_index = eval_strata * per_stratum + within
    placing = (slot_index[None, :] == jnp.arange(total_eval, dtype=jnp.int32)[:, None]).astype(
        jnp.bfloat16
    )
    grouped = jnp.dot(placing, gathered, preferred_element_type=jnp.float32).astype(jnp.bfloat16)
    block_pick = (block_strata[:, None] == jnp.arange(STRATA, dtype=jnp.int32)[None, :]).astype(
        jnp.bfloat16
    )
    chosen = jnp.dot(
        block_pick,
        grouped.reshape(STRATA, per_stratum * feature_cols),
        preferred_element_type=jnp.float32,
    )
    chosen = chosen.reshape(block_strata.shape[0], per_stratum, feature_cols)
    blocks = store_rows.reshape(block_strata.shape[0], BLOCK, feature_cols).astype(jnp.float32)
    block_scores = jnp.einsum("bpk,brk->bpr", chosen, blocks, precision=lax.Precision.HIGHEST)
    return (block_scores, within)


def expand_blocks(block_scores, within, own_strata, block_strata, row_count):
    per_stratum = block_scores.shape[1]
    picker = (within[:, None] == jnp.arange(per_stratum, dtype=jnp.int32)[None, :]).astype(
        jnp.float32
    )
    picked = jnp.einsum("bpr,ep->ber", block_scores, picker, precision=lax.Precision.HIGHEST)
    matched = own_strata[None, :, None] == block_strata[:, None, None]
    masked = jnp.where(matched, picked, jnp.zeros_like(picked))
    return jnp.transpose(masked, (1, 0, 2)).reshape(own_strata.shape[0], row_count)


def local(
    eval_inputs,
    eval_grads,
    w_gate,
    w_down,
    proj_in,
    proj_out,
    store_rows,
    eval_strata,
    block_strata,
):
    tokens = eval_inputs.shape[0]
    pieces = sent_together((w_gate, w_down.T), "store", 0, 1)
    gate_pre = add_columns(eval_inputs, pieces[0])
    back_pre = add_columns(eval_grads, pieces[1])
    update_bf = (back_pre * jax.nn.silu(gate_pre)).astype(jnp.bfloat16)
    right_part = jnp.dot(update_bf, proj_out, preferred_element_type=jnp.float32)
    seq_count = tokens // SEQ_LEN
    tensor_ways = lax.axis_size("tensor")
    quarter = RANK // tensor_ways
    left_proj = jnp.dot(eval_inputs, proj_in, preferred_element_type=jnp.float32)
    partial_outer = outer_mean(left_proj, right_part, seq_count)
    seq_grads = sent_and_summed(partial_outer, "tensor", 1)
    flat_grads = seq_grads.reshape(seq_count, quarter * RANK).astype(jnp.bfloat16)
    row_count = store_rows.shape[0]
    gathered = gather_directly(flat_grads, "store", 0)
    block_scores, within = stratum_blocks(gathered, eval_strata, block_strata, store_rows)
    summed = taken_together(block_scores, "tensor")
    own_count = gathered.shape[0] // tensor_ways
    own_start = lax.axis_index("tensor") * own_count
    own_within = lax.dynamic_slice_in_dim(within, own_start, own_count, 0)
    own_strata = lax.dynamic_slice_in_dim(eval_strata, own_start, own_count, 0)
    return expand_blocks(summed, own_within, own_strata, block_strata, row_count)


def solution(mesh):
    return jax.shard_map(
        local,
        mesh=mesh,
        in_specs=(
            P("store", None),
            P("store", None),
            P("store", "tensor"),
            P("tensor", "store"),
            P(),
            P("tensor", None),
            P("store", "tensor"),
            P(),
            P("store"),
        ),
        out_specs=P("tensor", "store"),
        check_vma=False,
    )
```

profile of v0, /device:TPU:1, one launch (start us, length us, event | category | flops | bytes accessed | tf_op | source)
XLA Modules:
  0.0 243.2 jit_solution(9717417885653700190)
XLA Ops:
  6.5 1.3 copy.23
  7.9 2.1 pad_maximum_fusion
  10.0 0.7 iota_compare_fusion.3
  10.7 0.6 reduce-window.6
  11.3 4.8 %convolution_bitcast_fusion.1 = f32[8,6,8,128]{3,2,1,0:T(8,128)S(1)} fusion(bf16[768,4096]{1,0:T(8,128)(2,1)} %param.9, bf16[4096,64]{0,1:T(8,128)(2,1)S(1)} %copy-done), kind=kOutput, calls=%fused_computation.18 | convolution fusion | flops 402653184 | bytes 7012352 | tf_op jit(solution)/shard_map/dot_general | solution.py:126
  16.1 112.2 %all-gather.2.cloned.1.call-done = bf16[4096,3584]{0,1:T(8,128)(2,1)} async-done(((bf16[128,3584]{0,1:T(8,128)(2,1)}), bf16[4096,3584]{0,1:T(8,128)(2,1)}) %all-gather.2.cloned.1.call-update) | async-done | bytes 29360144 | tf_op jit(solution)/shard_map/all_gather | solution.py:15
  128.3 17.6 %fusion.2 = f32[1792,768]{1,0:T(8,128)} fusion(bf16[768,4096]{1,0:T(8,128)(2,1)} %param.10, bf16[4096,3584]{0,1:T(8,128)(2,1)} %all-gather.2.cloned.1.call-done), kind=kOutput, calls=%fused_computation.2 | convolution fusion | flops 11274289152 | bytes 26476544 | tf_op jit(solution)/shard_map/dot_general | solution.py:52
  145.9 20.3 %convolution_bitcast_fusion = f32[8,6,8,128]{3,2,1,0:T(8,128)S(1)} fusion(bf16[1792,64]{0,1:T(8,128)(2,1)S(1)} %copy-done.4, f32[1792,768]{1,0:T(8,128)} %fusion.2, bf16[768,4096]{1,0:T(8,128)(2,1)} %param.9, bf16[4096,3584]{0,1:T(8,128)(2,1)} %all-gather.2.cloned.1.call-done), kind=kOutput, calls=%fused_computation.16 | convolution fusion | flops 11458707456 | bytes 26902528 | tf_op jit(solution)/shard_map/dot_general | solution.py:122
  166.2 0.4 convolution_multiply_fusion
  166.6 0.8 reshape.91
  167.4 4.0 %all-to-all-start = ((f32[4,1,6144]{2,1,0:T(1,128)}), f32[4,1,6144]{2,1,0:T(1,128)S(1)}, u32[]{:S(2)}, u32[]{:S(2)}) async-start(f32[4,1,6144]{2,1,0:T(1,128)} %reshape.91), calls=%async_computation | async-start | bytes 196608 | tf_op jit(solution)/shard_map/all_to_all | solution.py:26
  171.7 4.4 %all-to-all-done = f32[4,1,6144]{2,1,0:T(1,128)S(1)} async-done(((f32[4,1,6144]{2,1,0:T(1,128)}), f32[4,1,6144]{2,1,0:T(1,128)S(1)}, u32[]{:S(2)}, u32[]{:S(2)}) %all-to-all-start) | async-done | bytes 98336 | tf_op jit(solution)/shard_map/all_to_all | solution.py:26
  176.1 0.5 broadcast.51
  176.6 0.9 reduce.2
  177.8 0.9 broadcast_in_dim.12
  178.6 8.4 %all-to-all-start.1 = ((bf16[32,6,1024]{2,1,0:T(8,128)(2,1)}), bf16[32,6,1024]{2,1,0:T(8,128)(2,1)S(1)}, u32[]{:S(2)}, u32[]{:S(2)}) async-start(bf16[32,6,1024]{2,1,0:T(8,128)(2,1)} %broadcast_in_dim.12), calls=%async_computation.1 | async-start | bytes 1048576 | tf_op jit(solution)/shard_map/all_to_all | solution.py:32
  187.1 11.4 %all-to-all-done.1 = bf16[32,6,1024]{2,1,0:T(8,128)(2,1)S(1)} async-done(((bf16[32,6,1024]{2,1,0:T(8,128)(2,1)}), bf16[32,6,1024]{2,1,0:T(8,128)(2,1)S(1)}, u32[]{:S(2)}, u32[]{:S(2)}) %all-to-all-start.1) | async-done | bytes 393248 | tf_op jit(solution)/shard_map/all_to_all | solution.py:32
  199.2 0.6 fusion.25
  199.8 9.8 %fusion.11 = f32[32,24,128]{2,1,0:T(8,128)S(1)} fusion(bf16[32,128,1024]{2,1,0:T(8,128)(2,1)} %bitcast.77, f32[32,24,1024]{2,0,1:T(8,128)S(1)} %fusion.25), kind=kOutput, calls=%fused_computation.11 | convolution fusion | flops 1207959552 | bytes 11927552 | tf_op jit(solution)/shard_map/bpk,brk->bpr/dot_general | solution.py:91
  209.6 1.3 broadcast_in_dim.13
  210.8 3.6 %all-to-all-start.2 = ((f32[4,32,24,128]{3,2,1,0:T(8,128)}), f32[4,32,24,128]{3,2,1,0:T(8,128)S(1)}, u32[]{:S(2)}, u32[]{:S(2)}) async-start(f32[4,32,24,128]{3,2,1,0:T(8,128)} %broadcast_in_dim.13), calls=%async_computation.2 | async-start | bytes 3145728 | tf_op jit(solution)/shard_map/all_to_all | solution.py:32
  214.6 20.1 %all-to-all-done.2 = f32[4,32,24,128]{3,2,1,0:T(8,128)S(1)} async-done(((f32[4,32,24,128]{3,2,1,0:T(8,128)}), f32[4,32,24,128]{3,2,1,0:T(8,128)S(1)}, u32[]{:S(2)}, u32[]{:S(2)}) %all-to-all-start.2) | async-done | bytes 1572896 | tf_op jit(solution)/shard_map/all_to_all | solution.py:32
  234.9 0.6 fusion.13
  235.4 0.9 copy.44
  (30 shorter events, 1.6 us)
Async XLA Ops:
  6.5 4.7 %copy-start = (bf16[4096,64]{0,1:T(8,128)(2,1)S(1)}, bf16[4096,64]{0,1:T(8,128)(2,1)}, u32[]{:S(2)}) copy-start(bf16[4096,64]{0,1:T(8,128)(2,1)} %param.13) | copy-start | bytes 1572868
  6.5 121.7 %all-gather.2.cloned.1.call-start = ((), (), s32[]{:S(2)}) async-start(), calls=%async_computation.3 | async-start | bytes 30277632 | tf_op jit(solution)/shard_map/all_gather | solution.py:15
  16.1 129.8 %copy-start.4 = (bf16[1792,64]{0,1:T(8,128)(2,1)S(1)}, bf16[1792,64]{0,1:T(8,128)(2,1)}, u32[]{:S(2)}) copy-start(bf16[1792,64]{0,1:T(8,128)(2,1)} %param.14) | copy-start | bytes 688132
  145.9 41.2 %copy-start.2 = (s32[192]{0:T(256)S(1)}, s32[192]{0:T(256)}, u32[]{:S(2)}) copy-start(s32[192]{0:T(256)} %param.16) | copy-start | bytes 2308
  166.2 33.0 %copy-start.3 = (s32[32]{0:T(128)S(1)}, s32[32]{0:T(128)}, u32[]{:S(2)}) copy-start(s32[32]{0:T(128)} %param.17) | copy-start | bytes 388
  167.4 8.6 %all-to-all-start = ((f32[4,1,6144]{2,1,0:T(1,128)}), f32[4,1,6144]{2,1,0:T(1,128)S(1)}, u32[]{:S(2)}, u32[]{:S(2)}) async-start(f32[4,1,6144]{2,1,0:T(1,128)} %reshape.91), calls=%async_computation | async-start | bytes 196608 | tf_op jit(solution)/shard_map/all_to_all | solution.py:26
  178.6 19.9 %all-to-all-start.1 = ((bf16[32,6,1024]{2,1,0:T(8,128)(2,1)}), bf16[32,6,1024]{2,1,0:T(8,128)(2,1)S(1)}, u32[]{:S(2)}, u32[]{:S(2)}) async-start(bf16[32,6,1024]{2,1,0:T(8,128)(2,1)} %broadcast_in_dim.12), calls=%async_computation.1 | async-start | bytes 1048576 | tf_op jit(solution)/shard_map/all_to_all | solution.py:32
  199.8 36.6 %copy-start.1 = (bf16[4096,64]{0,1:T(8,128)(2,1)S(1)}, bf16[4096,64]{0,1:T(8,128)(2,1)}, u32[]{:S(2)}) copy-start(bf16[4096,64]{0,1:T(8,128)(2,1)} %param.13) | copy-start | bytes 1572868
  210.8 23.9 %all-to-all-start.2 = ((f32[4,32,24,128]{3,2,1,0:T(8,128)}), f32[4,32,24,128]{3,2,1,0:T(8,128)S(1)}, u32[]{:S(2)}, u32[]{:S(2)}) async-start(f32[4,32,24,128]{3,2,1,0:T(8,128)} %broadcast_in_dim.13), calls=%async_computation.2 | async-start | bytes 3145728 | tf_op jit(solution)/shard_map/all_to_all | solution.py:32
Sparse Core Ops, SparseCore 0:
  10.1 118.1 all-gather.1
where the time goes:
time: 244 us; the launch traced here: 243 us
  waiting for transfers between devices  148 us (61%)
  matrix products  54.3 us (22%)
  starting transfers between devices  15.9 us (7%)
  between operations  13.5 us (6%)
  local copies, waits for them, and re-layouts  6.66 us (3%)
  other arithmetic  4.6 us (2%)
    all_gather x1, waiting for transfers between devices, sent_together(): filled = lax.all_gather(both, axis, axis=dim, tiled=True)  112 us
    all_to_all x2, waiting for transfers between devices, from_everyone(): lax.all_to_all(jnp.broadcast_to(x[None], (length, *x.shape)), axis, 0, 0,...  31.5 us
    dot_general x1, matrix products, local(): jnp.dot(update_bf, proj_out, preferred_element_type=jnp.float32)  20.3 us
    dot_general x1, matrix products, add_columns(): return jnp.dot(source, block_piece, preferred_element_type=jnp.float32)  17.6 us
    all_to_all x2, starting transfers between devices, from_everyone(): lax.all_to_all(jnp.broadcast_to(x[None], (length, *x.shape)), axis, 0, 0,...  11.9 us
    dot_general x1, matrix products, stratum_blocks(): jnp.einsum('bpk,brk->bpr', chosen, blocks, precision=lax.Precision.HIGHEST)  9.77 us
  transfers between devices with their start and end apart: 4, of which 4 were waited for; matrix products, arithmetic and copies ran while one was open for 3% of the time, Pallas kernels for 0%

commit v1 on v0

v1 whole, which is shorter than its diff:
```python
import functools

import jax
import jax.numpy as jnp
from jax import lax
from jax.experimental import pallas as pl
from jax.experimental.pallas import tpu as pltpu
from jax.sharding import PartitionSpec as P

MESH = pl.DeviceIdType.MESH
RANK, SEQ, BLOCK, STRATA = 64, 128, 128, 8
PER = 24
PAD = 32
CHUNK = 256
AHEAD1, AHEAD2, AHEAD3, BEHIND, LATE = 6, 4, 2, 2, 3
BF16, F32, I32 = jnp.bfloat16, jnp.float32, jnp.int32
HIGH = lax.Precision.HIGHEST
NT = (((1,), (1,)), ((), ()))


def iota(shape, dim):
    return lax.broadcasted_iota(I32, shape, dim)


def kernel(
    x_in, g_in, wg_in, wd_in, pin_in, po_in, st_in, es_ref, bs_ref,
    out,
    wg, wd, xv, gv, st, raw, pin, po, po2, lt, right, pout, rbuf, gat, grouped, place, part, slot,
    lsem, osem, ssem, rsem, sibs, sibr, ysem, yrem, psem, prem, qsem, qrem, tsem, trem,
):
    chunks, tokens = wg.shape[0], xv.shape[0]
    seqs = tokens // SEQ
    s, t = lax.axis_index("store"), lax.axis_index("tensor")
    c, x, z = s % 2, (s // 2) % 4, s // 8

    def dev(zz, xx, cc):
        return (((zz % 4) * 4 + xx % 4) * 2 + cc, t)

    xm, xp, zm, zp = dev(z, x + 3, c), dev(z, x + 1, c), dev(z + 3, x, c), dev(z + 1, x, c)
    sib = dev(z, x, 1 - c)
    ypeer = [(s, (t + i) % 4) for i in (1, 2, 3)]

    barrier = pltpu.get_barrier_semaphore()
    for d in [xm, xp, zm, zp, sib] + ypeer:
        pl.semaphore_signal(barrier, inc=1, device_id=d, device_id_type=MESH)

    copy_raw = pltpu.make_async_copy(wd_in, raw, lsem.at[0])
    copy_raw.start()

    def own_gate(k):
        return pltpu.make_async_copy(
            wg_in.at[:, pl.ds(pl.multiple_of(k * CHUNK, CHUNK), CHUNK)], wg.at[k, c, z, x], osem.at[k]
        )

    for k in range(chunks):
        own_gate(k).start()

    def pieces(n, _):
        cc, hi, lo = n // 16, (n // 4) % 4, n % 4
        to = pl.ds(pl.multiple_of(n * 128, 128), 128)
        a = pl.ds(pl.multiple_of(((hi * 4 + lo) * 2 + cc) * 128, 128), 128)
        b = pl.ds(pl.multiple_of(((lo * 4 + hi) * 2 + cc) * 128, 128), 128)
        pltpu.make_async_copy(x_in.at[:, a], xv.at[:, to], lsem.at[1]).start()
        pltpu.make_async_copy(g_in.at[:, b], gv.at[:, to], lsem.at[2]).start()
        pltpu.make_async_copy(pin_in.at[a], pin.at[to], lsem.at[3]).start()
        return 0

    lax.fori_loop(0, 32, pieces, 0)
    copy_po = pltpu.make_async_copy(po_in, po, lsem.at[4])
    copy_po.start()
    copy_st = pltpu.make_async_copy(st_in, st, lsem.at[5])
    copy_st.start()

    copy_raw.wait()
    for k in range(chunks):
        wd[k, c, x, z] = raw[k * CHUNK : (k + 1) * CHUNK, :].T
    for k in range(chunks):
        own_gate(k).wait()
    pl.semaphore_wait(barrier, 8)

    def sides(ty):
        if ty == 0:
            return wg, z, x, xm, xp, zm, zp
        return wd, x, z, zm, zp, xm, xp

    def rc(ty, k, i, ref, d):
        return pltpu.make_async_remote_copy(
            src_ref=ref, dst_ref=ref, send_sem=ssem.at[ty, i], recv_sem=rsem.at[ty, i, k],
            device_id=d, device_id_type=MESH,
        )

    def msgs(ty, k):
        buf, a, b, bm, bp, am, ap = sides(ty)
        own = buf.at[k, c]
        am1, ap1, ap2 = (a + 3) % 4, (a + 1) % 4, (a + 2) % 4
        bm1, bp1, bp2 = (b + 3) % 4, (b + 1) % 4, (b + 2) % 4
        return (
            [(0, own.at[a, b], bp, own.at[a, bm1]), (1, own.at[a, b], bm, own.at[a, bp1])],
            [
                (2, own.at[a, bm1, 0:64], bp, own.at[a, bp2, 0:64]),
                (3, own.at[a, bp1, 64:128], bm, own.at[a, bp2, 64:128]),
            ],
            [(4, own.at[a], ap, own.at[am1]), (5, own.at[a], am, own.at[ap1])],
            [(6, own.at[am1, 0:2], ap, own.at[ap2, 0:2]), (7, own.at[ap1, 2:4], am, own.at[ap2, 2:4])],
        )

    def start(ty, k, phase):
        for i, ref, d, _ in msgs(ty, k)[phase]:
            rc(ty, k, i, ref, d).start()

    def arrived(ty, k, phase):
        for i, _, d, ref in msgs(ty, k)[phase]:
            rc(ty, k, i, ref, d).wait_recv()

    def shared(ty, k, i):
        buf, a, *_ = sides(ty)
        ref = buf.at[k, c, (a + (0, 3, 1, 2)[i]) % 4]
        return pltpu.make_async_remote_copy(
            src_ref=ref, dst_ref=ref, send_sem=sibs.at[ty, i], recv_sem=sibr.at[ty, k],
            device_id=sib, device_id_type=MESH,
        )

    def from_sibling(ty, k):
        ref = sides(ty)[0].at[k, 1 - c]
        return pltpu.make_async_remote_copy(
            src_ref=ref, dst_ref=ref, send_sem=sibs.at[ty, 0], recv_sem=sibr.at[ty, k],
            device_id=sib, device_id_type=MESH,
        )

    def within(k):
        return jnp.logical_and(k >= 0, k < chunks)

    def transfers(j):
        @pl.when(within(j + AHEAD1))
        def _():
            for ty in range(2):
                start(ty, j + AHEAD1, 0)

        @pl.when(within(j + AHEAD2))
        def _():
            for ty in range(2):
                arrived(ty, j + AHEAD2, 0)
                start(ty, j + AHEAD2, 1)

        @pl.when(within(j + AHEAD3))
        def _():
            for ty in range(2):
                arrived(ty, j + AHEAD3, 1)
                start(ty, j + AHEAD3, 2)
                shared(ty, j + AHEAD3, 0).start()

        @pl.when(within(j))
        def _():
            for ty in range(2):
                arrived(ty, j, 2)
                start(ty, j, 3)
                shared(ty, j, 1).start()
                shared(ty, j, 2).start()

        @pl.when(within(j - BEHIND))
        def _():
            for ty in range(2):
                arrived(ty, j - BEHIND, 3)
                shared(ty, j - BEHIND, 3).start()

    def hidden(k):
        for ty in range(2):
            from_sibling(ty, k).wait_recv()
        proj = po2[pl.ds(pl.multiple_of(k * CHUNK, CHUNK), CHUNK), :]

        def rows(m, _):
            at = pl.ds(pl.multiple_of(m * 256, 256), 256)
            gate = jnp.dot(xv[at, :], wg[k].reshape(4096, CHUNK), preferred_element_type=F32)
            back = jnp.dot(gv[at, :], wd[k].reshape(4096, CHUNK), preferred_element_type=F32)
            update = (back * (gate / (1.0 + jnp.exp(-gate)))).astype(BF16)
            right[at, :] += jnp.dot(update, proj, preferred_element_type=F32)
            return 0

        lax.fori_loop(0, tokens // 256, rows, 0)

    def before(j, _):
        transfers(j)
        return 0

    lax.fori_loop(-AHEAD1, 0, before, 0)

    right[...] = jnp.zeros_like(right)
    row = es_ref[...]
    col = jnp.sum(jnp.where(iota((192, 192), 0) == iota((192, 192), 1), row, 0), axis=1, keepdims=True)
    pos = iota((192, 256), 1)
    n, q = pos // 8, pos % 8
    ev = ((((n // 4) % 4) * 4 + n % 4) * 2 + n // 16) * 6 + q
    pick = jnp.logical_and(ev == iota((192, 256), 0), q < 6)
    stratum = jnp.sum(jnp.where(pick, col + 1, 0), axis=0, keepdims=True) - 1
    same = jnp.logical_and(row == col, iota((192, 192), 0) < iota((192, 192), 1))
    rank = jnp.sum(same.astype(I32), axis=0, keepdims=True)
    rank_col = jnp.sum(jnp.where(iota((192, 192), 0) == iota((192, 192), 1), rank, 0), axis=1, keepdims=True)
    slot[...] = col * PAD + rank_col
    target = jnp.sum(jnp.where(pick, col * PAD + rank_col, 0), axis=0, keepdims=True)
    target = jnp.where(stratum >= 0, target, -1)
    place[...] = (iota((256, 256), 0) == target).astype(F32).astype(BF16)
    copy_po.wait()
    po2[...] = jnp.concatenate([po[...], po[...]], axis=1)
    pltpu.make_async_copy(x_in, xv, lsem.at[1]).wait()
    pltpu.make_async_copy(pin_in, pin, lsem.at[3]).wait()
    halves = iota((64, 64), 1)
    order = (iota((64, 64), 0) == jnp.where(halves < 32, 2 * halves, 2 * halves - 63)).astype(F32)

    def left_rows(m, _):
        at = pl.ds(pl.multiple_of(m * SEQ, SEQ), SEQ)
        left = jnp.dot(xv[at, :], pin[...], preferred_element_type=F32)
        left = jnp.dot(left, order, precision=HIGH, preferred_element_type=F32)
        lt[m] = left.T
        return 0

    lax.fori_loop(0, seqs, left_rows, 0)
    pltpu.make_async_copy(g_in, gv, lsem.at[2]).wait()
    copy_st.wait()

    def steady(j, _):
        transfers(j)

        @pl.when(within(j - LATE))
        def _():
            hidden(j - LATE)

        return 0

    lax.fori_loop(0, chunks + LATE, steady, 0)

    lane = iota((32, 128), 1)
    for m in range(seqs):
        both = jnp.dot(lt[m], right[m * SEQ : (m + 1) * SEQ, :], precision=HIGH, preferred_element_type=F32)
        flat = jnp.where(lane < 64, both[0:32], both[32:64])
        for u in range(4):
            pout[u, m] = flat[u * 8 : u * 8 + 8]

    def quarter(i, to, at):
        return pltpu.make_async_remote_copy(
            src_ref=pout.at[to], dst_ref=rbuf.at[at], send_sem=ysem.at[i], recv_sem=yrem.at[i],
            device_id=(s, to), device_id_type=MESH,
        )

    for i in range(3):
        quarter(i, (t + i + 1) % 4, t).start()
    total = pout[t]
    for i in range(3):
        quarter(i, (t + i + 1) % 4, (t + 3 - i) % 4).wait_recv()
        total += rbuf[(t + 3 - i) % 4]
    mine = (total * (1.0 / SEQ)).reshape(seqs * 8, 128).astype(BF16)
    to, fr = iota((64, 48), 0), iota((64, 48), 1)
    turn = jnp.logical_and(fr // 8 == to % 8, fr % 8 == to // 8).astype(F32).astype(BF16)
    gat[c, z, x] = jnp.dot(turn, mine, preferred_element_type=F32).astype(BF16)

    def flat_copy(i, zz, xx):
        return pltpu.make_async_remote_copy(
            src_ref=gat.at[c, zz, xx], dst_ref=gat.at[c, zz, xx], send_sem=psem.at[i], recv_sem=prem.at[i],
            device_id=dev(z + i // 4, x + i % 4, c), device_id_type=MESH,
        )

    for i in (10, 6, 14, 9, 11, 2, 8, 5, 7, 13, 15, 1, 3, 4, 12):
        flat_copy(i, z, x).start()
    for i in (1, 3, 4, 12, 5, 7, 13, 15, 2, 8, 6, 14, 9, 11, 10):
        flat_copy(i, (z + 4 - i // 4) % 4, (x + 4 - i % 4) % 4).wait_recv()

    def flat_shared(cc):
        return pltpu.make_async_remote_copy(
            src_ref=gat.at[cc], dst_ref=gat.at[cc], send_sem=tsem, recv_sem=trem,
            device_id=sib, device_id_type=MESH,
        )

    flat_shared(c).start()
    flat_shared(1 - c).wait_recv()
    flats = gat[...].reshape(32, 64, 128).astype(F32)
    for kk in range(8):
        some = flats[:, kk * 8 : kk * 8 + 8, :].reshape(256, 128).astype(BF16)
        rows = jnp.dot(place[...], some, preferred_element_type=F32).astype(BF16)
        grouped[:, :, kk * 128 : (kk + 1) * 128] = rows.reshape(STRATA, PAD, 128)

    def part_copy(g, i, to, at):
        ref = part.at[at, pl.ds(g * 4, 4)]
        return pltpu.make_async_remote_copy(
            src_ref=ref, dst_ref=ref, send_sem=qsem.at[g, i], recv_sem=qrem.at[g, i],
            device_id=(s, to), device_id_type=MESH,
        )

    def group(g, _):
        def pair(p, _):
            m = g * 4 + p
            two = []
            for e in range(2):
                b = 2 * m + e
                stored = st[pl.ds(pl.multiple_of(b * BLOCK, BLOCK), BLOCK), :]
                chosen = grouped[bs_ref[b]]
                two.append(lax.dot_general(chosen, stored, NT, preferred_element_type=F32)[0:PER])
            part[t, m] = jnp.concatenate(two, axis=0).astype(BF16)
            return 0

        lax.fori_loop(0, 4, pair, 0)
        for i in range(3):
            part_copy(g, i, (t + i + 1) % 4, t).start()
        return 0

    lax.fori_loop(0, 4, group, 0)

    own = slot[pl.ds(pl.multiple_of(t * 48, 8), 48), :]
    own = jnp.concatenate([own, own], axis=0)
    half = iota((96, 192), 0) // 48
    entry = iota((96, 192), 1) % 48
    block_of, rank_of = entry // PER, entry % PER

    def expand(g, _):
        for i in range(3):
            part_copy(g, i, (t + i + 1) % 4, (t + 3 - i) % 4).wait_recv()

        def pair(p, _):
            m = g * 4 + p
            strata = jnp.where(block_of == 0, bs_ref[2 * m], bs_ref[2 * m + 1])
            chosen = jnp.logical_and(own == strata * PAD + rank_of, half == block_of)
            summed = jnp.dot(
                chosen.astype(F32).astype(BF16), part[:, m].reshape(192, 128), preferred_element_type=F32
            )
            out[:, pl.ds(pl.multiple_of(m * 256, 256), 256)] = jnp.concatenate([summed[0:48], summed[48:96]], axis=1)
            return 0

        lax.fori_loop(0, 4, pair, 0)
        return 0

    lax.fori_loop(0, 4, expand, 0)

    for ty in range(2):
        buf, a, b, bm, bp, am, ap = sides(ty)
        own_buf = buf.at[:, c]
        sizes = [
            own_buf.at[:, a, b], own_buf.at[:, a, b], own_buf.at[:, a, b, 0:64], own_buf.at[:, a, b, 0:64],
            own_buf.at[:, a], own_buf.at[:, a], own_buf.at[:, a, 0:2], own_buf.at[:, a, 0:2],
        ]
        for i, ref in enumerate(sizes):
            rc(ty, 0, i, ref, xm).wait_send()
        for i in range(4):
            ref = own_buf.at[:, a]
            pltpu.make_async_remote_copy(
                src_ref=ref, dst_ref=ref, send_sem=sibs.at[ty, i], recv_sem=sibr.at[ty, 0],
                device_id=sib, device_id_type=MESH,
            ).wait_send()
    for i in range(3):
        quarter(i, (t + i + 1) % 4, t).wait_send()
    for i in range(1, 16):
        flat_copy(i, z, x).wait_send()
    flat_shared(c).wait_send()
    for g in range(4):
        for i in range(3):
            part_copy(g, i, (t + i + 1) % 4, t).wait_send()


def local(eval_inputs, eval_grads, w_gate, w_down, proj_in, proj_out, store_rows, eval_strata, block_strata):
    tokens, width = eval_inputs.shape
    cols = w_gate.shape[1]
    chunks = cols // CHUNK
    rows, feats = store_rows.shape
    any_space = pl.BlockSpec(memory_space=pl.ANY)
    dma = pltpu.SemaphoreType.DMA
    evals = eval_strata.shape[0]
    seqs = tokens // SEQ
    return pl.pallas_call(
        kernel,
        out_shape=jax.ShapeDtypeStruct((evals // 4, rows), F32),
        in_specs=[any_space] * 7
        + [pl.BlockSpec(memory_space=pltpu.VMEM), pl.BlockSpec(memory_space=pltpu.SMEM)],
        out_specs=pl.BlockSpec(memory_space=pltpu.VMEM),
        scratch_shapes=[
            pltpu.VMEM((chunks, 2, 4, 4, 128, CHUNK), BF16),
            pltpu.VMEM((chunks, 2, 4, 4, 128, CHUNK), BF16),
            pltpu.VMEM((tokens, width), BF16),
            pltpu.VMEM((tokens, width), BF16),
            pltpu.VMEM((rows, feats), BF16),
            pltpu.VMEM((cols, 128), BF16),
            pltpu.VMEM((width, RANK), BF16),
            pltpu.VMEM((cols, RANK), BF16),
            pltpu.VMEM((cols, 2 * RANK), BF16),
            pltpu.VMEM((seqs, RANK, SEQ), F32),
            pltpu.VMEM((tokens, 2 * RANK), F32),
            pltpu.VMEM((4, seqs, 8, 128), F32),
            pltpu.VMEM((4, seqs, 8, 128), F32),
            pltpu.VMEM((2, 4, 4, 64, 128), BF16),
            pltpu.VMEM((STRATA, PAD, feats), BF16),
            pltpu.VMEM((256, 256), BF16),
            pltpu.VMEM((4, rows // (2 * BLOCK), 2 * PER, BLOCK), BF16),
            pltpu.VMEM((evals, 1), I32),
            dma((6,)),
            dma((chunks,)),
            dma((2, 8)),
            dma((2, 8, chunks)),
            dma((2, 4)),
            dma((2, chunks)),
            dma((3,)),
            dma((3,)),
            dma((16,)),
            dma((16,)),
            dma((4, 3)),
            dma((4, 3)),
            dma,
            dma,
        ],
        compiler_params=pltpu.CompilerParams(
            collective_id=0, has_side_effects=True, vmem_limit_bytes=64 * 2**20 - 2**19
        ),
    )(
        eval_inputs, eval_grads, w_gate, w_down, proj_in, proj_out, store_rows,
        eval_strata.reshape(1, evals), block_strata,
    )


def solution(mesh):
    return jax.shard_map(
        local,
        mesh=mesh,
        in_specs=(
            P("store", None),
            P("store", None),
            P("store", "tensor"),
            P("tensor", "store"),
            P(),
            P("tensor", None),
            P("store", "tensor"),
            P(),
            P("store"),
        ),
        out_specs=P("tensor", "store"),
        check_vma=False,
    )
```

time: 244 us -> 131 us (0.54)
  waiting for transfers between devices: 148 us -> 0 us
  Pallas kernels: 0 us -> 124 us
  matrix products: 54.3 us -> 0 us
  starting transfers between devices: 15.9 us -> 0 us
  between operations: 13.5 us -> 0.01 us
  other arithmetic: 4.6 us -> 0 us
    pallas_call x0 -> x1, Pallas kernels: none -> 124 us  [local(): pl.pallas_call(kernel, out_shape=jax.ShapeDtypeStruct((evals // 4, rows),...]
    all_gather x1 -> x0, waiting for transfers between devices: 112 us -> none  [sent_together(): filled = lax.all_gather(both, axis, axis=dim, tiled=True)]
    dot_general x8 -> x0, matrix products: 54.3 us -> none  [the longest x1 20.3 us: local(): jnp.dot(update_bf, proj_out, preferred_element_type=jnp.float32)]
    all_to_all x3 -> x0, waiting for transfers between devices: 35.9 us -> none  [the longest x2 31.5 us: from_everyone(): lax.all_to_all(jnp.broadcast_to(x[None], (length, *x.shape)), axis, 0, 0,...]
    all_to_all x3 -> x0, starting transfers between devices: 15.9 us -> none  [the longest x2 11.9 us: from_everyone(): lax.all_to_all(jnp.broadcast_to(x[None], (length, *x.shape)), axis, 0, 0,...]
    unnamed x13 -> x3, local copies, waits for them, and re-layouts: 2.31 us -> 6.35 us
  transfers between devices with their start and end apart: 4 -> 0, of which waited for: 4 -> 0; matrix products, arithmetic and copies ran while one was open for 3% -> 0% of each run, Pallas kernels for 0% -> 0%
where the time goes in v1:
time: 131 us; the launch traced here: 130 us
  Pallas kernels  124 us (95%)
  local copies, waits for them, and re-layouts  6.35 us (5%)
    pallas_call x1, Pallas kernels, local(): pl.pallas_call(kernel, out_shape=jax.ShapeDtypeStruct((evals // 4, rows),...  124 us
    unnamed x3, local copies, waits for them, and re-layouts  6.35 us

profile of v1, /device:TPU:1, one launch (start us, length us, event | category | flops | bytes accessed | tf_op | source)
XLA Modules:
  0.0 130.3 jit_solution(13959564771752750319)
XLA Ops:
  0.0 1.9 %copy.11.po_in = bf16[1792,64]{1,0:T(8,128)(2,1)} copy(bf16[1792,64]{0,1:T(8,128)(2,1)} %param.14) | data formatting | bytes 458752 | tf_op args[5]
  1.9 2.4 %copy.10.pin_in = bf16[4096,64]{1,0:T(8,128)(2,1)} copy(bf16[4096,64]{0,1:T(8,128)(2,1)} %param.13) | data formatting | bytes 1048576 | tf_op args[4]
  4.3 123.9 %shard_map.91 = f32[48,4096]{1,0:T(8,128)} custom-call(bf16[768,4096]{1,0:T(8,128)(2,1)} %x_in.1, bf16[768,4096]{1,0:T(8,128)(2,1)} %g_in.1, bf16[128,1792]{1,0:T(8,128)(2,1)} %wg_in.1, bf16[1792,128]{1,0:T(8,128)(2,1)} %wd_in.1, bf16[4096,64]{1,0:T(8,128)(2,1)} %copy.10.pin_in, bf16[1792,64]{1,0:T(8,128)(2,1)} %copy.11.po_in, bf16[4096,1024]{1,0:T(8,128)(2,1)} %st_in.1, ...), custom_call_target="tpu_custom_call" | custom-call | tf_op jit(solution)/shard_map/pallas_call | solution.py:365
  128.2 2.1 %copy.13 = f32[48,4096]{1,0:T(8,128)} copy(f32[48,4096]{1,0:T(8,128)} %shard_map.91) | data formatting | bytes 1572864

commit v2 on v1

v2 whole, which is shorter than its diff:
```python
import functools

import jax
import jax.numpy as jnp
from jax import lax
from jax.experimental import pallas as pl
from jax.experimental.pallas import tpu as pltpu
from jax.sharding import PartitionSpec as P

MESH = pl.DeviceIdType.MESH
RANK, SEQ, BLOCK, STRATA = 64, 128, 128, 8
PAD = 32
CHUNK = 256
AHEAD1, AHEAD2, AHEAD3 = 6, 4, 2
ORDER = "edrabRcmM"
TILE = 384
BF16, F32, I32 = jnp.bfloat16, jnp.float32, jnp.int32
HIGH = lax.Precision.HIGHEST
NT = (((1,), (1,)), ((), ()))


def iota(shape, dim):
    return lax.broadcasted_iota(I32, shape, dim)


def kernel(
    x_in, g_in, wg_in, wd_in, pin_in, po_in, st_in, es_ref, bs_ref,
    out,
    wg, wd, xv, gv, st, raw, pin, po, po2, lt, acc, right, pout, rbuf, gat, grouped, place, part, got, full, slot,
    lsem, osem, ssem, rsem, sibs, sibr, ysem, yrem, psem, prem, qsem, qrem, fsem, frem, tsem, trem,
):
    chunks, tokens = wg.shape[0], xv.shape[0]
    seqs = tokens // SEQ
    s, t = lax.axis_index("store"), lax.axis_index("tensor")
    c, x, z = s % 2, (s // 2) % 4, s // 8

    def dev(zz, xx, cc):
        return (((zz % 4) * 4 + xx % 4) * 2 + cc, t)

    xm, xp, zm, zp = dev(z, x + 3, c), dev(z, x + 1, c), dev(z + 3, x, c), dev(z + 1, x, c)
    sib = dev(z, x, 1 - c)
    ypeer = [(s, (t + i) % 4) for i in (1, 2, 3)]

    barrier = pltpu.get_barrier_semaphore()
    for d in [xm, xp, zm, zp, sib] + ypeer:
        pl.semaphore_signal(barrier, inc=1, device_id=d, device_id_type=MESH)

    copy_raw = pltpu.make_async_copy(wd_in, raw, lsem.at[0])
    copy_raw.start()

    def own_gate(k):
        return pltpu.make_async_copy(
            wg_in.at[:, pl.ds(pl.multiple_of(k * CHUNK, CHUNK), CHUNK)], wg.at[k, c, z, x], osem.at[k]
        )

    for k in range(chunks):
        own_gate(k).start()

    copy_raw.wait()
    for k in range(chunks):
        wd[k, c, x, z] = raw[k * CHUNK : (k + 1) * CHUNK, :].T
    for k in range(chunks):
        own_gate(k).wait()
    pl.semaphore_wait(barrier, 8)

    def pieces(n, _):
        cc, hi, lo = n // 16, (n // 4) % 4, n % 4
        to = pl.ds(pl.multiple_of(n * 128, 128), 128)
        a = pl.ds(pl.multiple_of(((hi * 4 + lo) * 2 + cc) * 128, 128), 128)
        b = pl.ds(pl.multiple_of(((lo * 4 + hi) * 2 + cc) * 128, 128), 128)
        pltpu.make_async_copy(x_in.at[:, a], xv.at[:, to], lsem.at[1]).start()
        pltpu.make_async_copy(g_in.at[:, b], gv.at[:, to], lsem.at[2]).start()
        pltpu.make_async_copy(pin_in.at[:, a], pin.at[:, to], lsem.at[3]).start()
        return 0

    copy_po = pltpu.make_async_copy(po_in, po, lsem.at[4])
    copy_st = pltpu.make_async_copy(st_in, st, lsem.at[5])

    def loads():
        copy_po.start()
        lax.fori_loop(0, 32, pieces, 0)
        copy_st.start()

    def sides(ty):
        if ty == 0:
            return wg, z, x, xm, xp, zm, zp
        return wd, x, z, zm, zp, xm, xp

    def rc(ty, k, i, ref, d):
        return pltpu.make_async_remote_copy(
            src_ref=ref, dst_ref=ref, send_sem=ssem.at[ty, i], recv_sem=rsem.at[ty, i, k],
            device_id=d, device_id_type=MESH,
        )

    def msgs(ty, k):
        buf, a, b, bm, bp, am, ap = sides(ty)
        own = buf.at[k, c]
        am1, ap1, ap2 = (a + 3) % 4, (a + 1) % 4, (a + 2) % 4
        bm1, bp1, bp2 = (b + 3) % 4, (b + 1) % 4, (b + 2) % 4
        return (
            [(0, own.at[a, b], bp, own.at[a, bm1]), (1, own.at[a, b], bm, own.at[a, bp1])],
            [
                (2, own.at[a, bm1, 0:64], bp, own.at[a, bp2, 0:64]),
                (3, own.at[a, bp1, 64:128], bm, own.at[a, bp2, 64:128]),
            ],
            [(4, own.at[a], ap, own.at[am1]), (5, own.at[a], am, own.at[ap1])],
            [(6, own.at[am1, 0:2], ap, own.at[ap2, 0:2]), (7, own.at[ap1, 2:4], am, own.at[ap2, 2:4])],
        )

    def start(ty, k, phase):
        for i, ref, d, _ in msgs(ty, k)[phase]:
            rc(ty, k, i, ref, d).start()

    def arrived(ty, k, phase):
        for i, _, d, ref in msgs(ty, k)[phase]:
            rc(ty, k, i, ref, d).wait_recv()

    def shared(ty, k, i):
        buf, a, *_ = sides(ty)
        ref = buf.at[k, c, (a + (0, 3, 1, 2)[i]) % 4]
        return pltpu.make_async_remote_copy(
            src_ref=ref, dst_ref=ref, send_sem=sibs.at[ty, i], recv_sem=sibr.at[ty, i // 3, k],
            device_id=sib, device_id_type=MESH,
        )

    def from_sibling(ty, k, last):
        ref = sides(ty)[0].at[k, 1 - c, 3:4] if last else sides(ty)[0].at[k, 1 - c, 0:3]
        return pltpu.make_async_remote_copy(
            src_ref=ref, dst_ref=ref, send_sem=sibs.at[ty, 0], recv_sem=sibr.at[ty, last, k],
            device_id=sib, device_id_type=MESH,
        )

    def within(k):
        if isinstance(k, int):
            return lambda f: f() if 0 <= k < chunks else None
        return pl.when(jnp.logical_and(k >= 0, k < chunks))

    def first_hop(j):
        @within(j + AHEAD1)
        def _():
            for ty in range(2):
                start(ty, j + AHEAD1, 0)

    def second_hop(j):
        @within(j + AHEAD2)
        def _():
            for ty in range(2):
                arrived(ty, j + AHEAD2, 0)
                start(ty, j + AHEAD2, 1)

    def third_hop(j):
        @within(j + AHEAD3)
        def _():
            for ty in range(2):
                arrived(ty, j + AHEAD3, 1)
                start(ty, j + AHEAD3, 2)
                shared(ty, j + AHEAD3, 0).start()

    def fourth_hop(j):
        @within(j)
        def _():
            for ty in range(2):
                arrived(ty, j, 2)
                start(ty, j, 3)
                shared(ty, j, 1).start()
                shared(ty, j, 2).start()

    def last_line(j):
        @within(j - 1)
        def _():
            for ty in range(2):
                arrived(ty, j - 1, 3)
                shared(ty, j - 1, 3).start()

    def product(at, ty, k, lines):
        lhs, rhs = (xv, wg) if ty == 0 else (gv, wd)
        total = None
        for line in lines:
            for cc in range(2):
                cols = pl.ds(pl.multiple_of((cc * 4 + line) * 512, 512), 512)
                term = jnp.dot(lhs[at, cols], rhs[k, cc, line].reshape(512, CHUNK), preferred_element_type=F32)
                total = term if total is None else total + term
        return total

    def most(j, part):
        @within(j)
        def _():
            at = pl.ds(part * TILE, TILE)
            for ty in range(2):
                if part == 0:
                    from_sibling(ty, j, 0).wait_recv()
            for ty in range(2):
                a = (z, x)[ty]
                acc[ty, at, :] = product(at, ty, j, [a, (a + 1) % 4, (a + 3) % 4])

    def rest(j, part):
        @within(j - 1)
        def _():
            k = j - 1
            at = pl.ds(part * TILE, TILE)
            for ty in range(2):
                if part == 0:
                    from_sibling(ty, k, 1).wait_recv()
            proj = po2[pl.ds(pl.multiple_of(k * CHUNK, CHUNK), CHUNK), :]
            gate = acc[0, at, :] + product(at, 0, k, [(z + 2) % 4])
            back = acc[1, at, :] + product(at, 1, k, [(x + 2) % 4])
            update = (back * (gate / (1.0 + jnp.exp(-gate)))).astype(BF16)
            right[at, :] += jnp.dot(update, proj, preferred_element_type=F32)

    def tables():
        row = es_ref[...]
        diag = iota((192, 192), 0) == iota((192, 192), 1)
        col = jnp.sum(jnp.where(diag, row, 0), axis=1, keepdims=True)
        same = jnp.logical_and(row == col, iota((192, 192), 0) < iota((192, 192), 1))
        rank = jnp.sum(same.astype(I32), axis=0, keepdims=True)
        rank = jnp.sum(jnp.where(diag, rank, 0), axis=1, keepdims=True)
        here = col * PAD + (rank // 6) * 8 + rank % 6
        slot[...] = here
        pos = iota((192, 256), 1)
        n, q = pos // 8, pos % 8
        ev = ((((n // 4) % 4) * 4 + n % 4) * 2 + n // 16) * 6 + q
        pick = jnp.logical_and(ev == iota((192, 256), 0), q < 6)
        target = jnp.sum(jnp.where(pick, here + 1, 0), axis=0, keepdims=True) - 1
        place[...] = (iota((256, 256), 0) == target).astype(F32).astype(BF16)

    def projections():
        right[...] = jnp.zeros_like(right)
        copy_po.wait()
        side = po[...].T
        po2[...] = jnp.concatenate([side, side], axis=1)
        pltpu.make_async_copy(x_in, xv, lsem.at[1]).wait()
        pltpu.make_async_copy(pin_in, pin, lsem.at[3]).wait()
        to = iota((64, 64), 0)
        order = (iota((64, 64), 1) == jnp.where(to < 32, 2 * to, 2 * to - 63)).astype(F32).astype(BF16)
        pin[...] = jnp.dot(order, pin[...], preferred_element_type=F32).astype(BF16)

    def lefts(m):
        lt[m] = lax.dot_general(pin[...], xv[m * SEQ : (m + 1) * SEQ, :], NT, preferred_element_type=F32)

    work = {
        0: [loads],
        1: [tables],
        2: [projections],
    }
    for m in range(seqs):
        work.setdefault(3 + m // 2, []).append(functools.partial(lefts, m))
    for j in range(AHEAD1):
        for f in (first_hop, second_hop, third_hop):
            f(j - AHEAD1)
        for f in work.get(j, []):
            f()
    pltpu.make_async_copy(g_in, gv, lsem.at[2]).wait()
    copy_st.wait()

    steps = {
        "a": first_hop, "b": second_hop, "c": third_hop, "d": fourth_hop, "e": last_line,
        "m": functools.partial(most, part=0), "M": functools.partial(most, part=1),
        "r": functools.partial(rest, part=0), "R": functools.partial(rest, part=1),
    }

    def steady(j, _):
        for name in ORDER:
            steps[name](j)
        return 0

    lax.fori_loop(0, chunks + 1, steady, 0)

    lane = iota((32, 128), 1)
    for m in range(seqs):
        both = jnp.dot(lt[m], right[m * SEQ : (m + 1) * SEQ, :], precision=HIGH, preferred_element_type=F32)
        flat = jnp.where(lane < 64, both[0:32], both[32:64])
        for u in range(4):
            pout[u, m] = flat[u * 8 : u * 8 + 8]

    def quarter(i, to, at):
        return pltpu.make_async_remote_copy(
            src_ref=pout.at[to], dst_ref=rbuf.at[at], send_sem=ysem.at[i], recv_sem=yrem.at[i],
            device_id=(s, to), device_id_type=MESH,
        )

    for i in range(3):
        quarter(i, (t + i + 1) % 4, t).start()
    total = pout[t]
    for i in range(3):
        quarter(i, (t + i + 1) % 4, (t + 3 - i) % 4).wait_recv()
        total += rbuf[(t + 3 - i) % 4]
    mine = (total * (1.0 / SEQ)).reshape(seqs * 8, 128).astype(BF16)
    to, fr = iota((64, 48), 0), iota((64, 48), 1)
    turn = jnp.logical_and(fr // 8 == to % 8, fr % 8 == to // 8).astype(F32).astype(BF16)
    gat[c, z, x] = jnp.dot(turn, mine, preferred_element_type=F32).astype(BF16)

    def flat_copy(i, zz, xx):
        return pltpu.make_async_remote_copy(
            src_ref=gat.at[c, zz, xx], dst_ref=gat.at[c, zz, xx], send_sem=psem.at[i], recv_sem=prem.at[i],
            device_id=dev(z + i // 4, x + i % 4, c), device_id_type=MESH,
        )

    for i in (10, 6, 14, 9, 11, 2, 8, 5, 7, 13, 15, 1, 3, 4, 12):
        flat_copy(i, z, x).start()

    def flat_shared(ref):
        return pltpu.make_async_remote_copy(
            src_ref=ref, dst_ref=ref, send_sem=tsem, recv_sem=trem, device_id=sib, device_id_type=MESH
        )

    flat_shared(gat.at[c, z, x]).start()
    for i in (1, 3, 4, 12, 5, 7, 13, 15, 2, 8, 6, 14, 9, 11, 10):
        zz, xx = (z + 4 - i // 4) % 4, (x + 4 - i % 4) % 4
        flat_copy(i, zz, xx).wait_recv()
        flat_shared(gat.at[c, zz, xx]).start()
    flat_shared(gat.at[1 - c]).wait_recv()
    flats = gat[...].reshape(32, 64, 128).astype(F32)
    for kk in range(8):
        some = flats[:, kk * 8 : kk * 8 + 8, :].reshape(256, 128).astype(BF16)
        rows = jnp.dot(place[...], some, preferred_element_type=F32).astype(BF16)
        grouped[:, :, kk * 128 : (kk + 1) * 128] = rows.reshape(STRATA, PAD, 128)

    def part_copy(g, i, to, at):
        some = pl.ds(g * 8, 8)
        return pltpu.make_async_remote_copy(
            src_ref=part.at[to, some], dst_ref=got.at[at, some], send_sem=qsem.at[g, i], recv_sem=qrem.at[g, i],
            device_id=(s, to), device_id_type=MESH,
        )

    def full_copy(g, i, to, at):
        ref = full.at[at, pl.ds(g * 8, 8)]
        return pltpu.make_async_remote_copy(
            src_ref=ref, dst_ref=ref, send_sem=fsem.at[g, i], recv_sem=frem.at[g, i],
            device_id=(s, to), device_id_type=MESH,
        )

    for g in range(2):

        def blocks(p, _):
            first = g * 8 + p * 4
            found = []
            for e in range(8):
                b = 2 * first + e
                stored = st[pl.ds(pl.multiple_of(b * BLOCK, BLOCK), BLOCK), :]
                found.append(lax.dot_general(grouped[bs_ref[b]], stored, NT, preferred_element_type=F32))
            for m in range(4):
                for u in range(4):
                    both = [r[u * 8 : u * 8 + 8] for r in found[2 * m : 2 * m + 2]]
                    part[u, first + m] = jnp.concatenate(both, axis=0).astype(BF16)
            return 0

        lax.fori_loop(0, 2, blocks, 0)
        for i in range(3):
            part_copy(g, i, (t + i + 1) % 4, t).start()
    for g in range(2):
        for i in range(3):
            part_copy(g, i, (t + i + 1) % 4, (t + 3 - i) % 4).wait_recv()
        some = pl.ds(g * 8, 8)
        total = part[t, some].astype(F32)
        for i in range(3):
            total += got[(t + 3 - i) % 4, some].astype(F32)
        full[t, some] = total.astype(BF16)
        for i in range(3):
            full_copy(g, i, (t + i + 1) % 4, t).start()

    own = slot[pl.ds(pl.multiple_of(t * 48, 8), 48), :]
    entry = iota((96, 64), 1)
    block_of = (entry // 8) % 2
    rest_of = jnp.concatenate([own, own], axis=0) - (entry // 16) * 8 - entry % 8
    rest_of = jnp.where(iota((96, 64), 0) // 48 == block_of, rest_of, -1)
    for g in range(2):
        for i in range(3):
            full_copy(g, i, (t + i + 1) % 4, (t + 3 - i) % 4).wait_recv()

        def expand(p, _):
            for e in range(4):
                m = g * 8 + p * 4 + e
                chosen = rest_of == jnp.where(block_of == 0, bs_ref[2 * m] * PAD, bs_ref[2 * m + 1] * PAD)
                summed = jnp.dot(
                    chosen.astype(F32).astype(BF16), full[:, m].reshape(64, 128), preferred_element_type=F32
                )
                at = pl.multiple_of(m * 2 * BLOCK, 2 * BLOCK)
                out[:, pl.ds(at, BLOCK)] = summed[0:48]
                out[:, pl.ds(at + BLOCK, BLOCK)] = summed[48:96]
            return 0

        lax.fori_loop(0, 2, expand, 0)

    for ty in range(2):
        buf, a, b, bm, bp, am, ap = sides(ty)
        own_buf = buf.at[:, c]
        sizes = [
            own_buf.at[:, a, b], own_buf.at[:, a, b], own_buf.at[:, a, b, 0:64], own_buf.at[:, a, b, 0:64],
            own_buf.at[:, a], own_buf.at[:, a], own_buf.at[:, a, 0:2], own_buf.at[:, a, 0:2],
        ]
        for i, ref in enumerate(sizes):
            rc(ty, 0, i, ref, xm).wait_send()
        for i in range(4):
            ref = own_buf.at[:, a]
            pltpu.make_async_remote_copy(
                src_ref=ref, dst_ref=ref, send_sem=sibs.at[ty, i], recv_sem=sibr.at[ty, 0, 0],
                device_id=sib, device_id_type=MESH,
            ).wait_send()
    for i in range(3):
        quarter(i, (t + i + 1) % 4, t).wait_send()
    for i in range(1, 16):
        flat_copy(i, z, x).wait_send()
    flat_shared(gat.at[c]).wait_send()
    for g in range(2):
        for i in range(3):
            part_copy(g, i, (t + i + 1) % 4, t).wait_send()
            full_copy(g, i, (t + i + 1) % 4, t).wait_send()


def local(eval_inputs, eval_grads, w_gate, w_down, proj_in, proj_out, store_rows, eval_strata, block_strata):
    tokens, width = eval_inputs.shape
    cols = w_gate.shape[1]
    chunks = cols // CHUNK
    rows, feats = store_rows.shape
    any_space = pl.BlockSpec(memory_space=pl.ANY)
    dma = pltpu.SemaphoreType.DMA
    evals = eval_strata.shape[0]
    seqs = tokens // SEQ
    return pl.pallas_call(
        kernel,
        out_shape=jax.ShapeDtypeStruct((evals // 4, rows), F32),
        in_specs=[any_space] * 7
        + [pl.BlockSpec(memory_space=pltpu.VMEM), pl.BlockSpec(memory_space=pltpu.SMEM)],
        out_specs=pl.BlockSpec(memory_space=pltpu.VMEM),
        scratch_shapes=[
            pltpu.VMEM((chunks, 2, 4, 4, 128, CHUNK), BF16),
            pltpu.VMEM((chunks, 2, 4, 4, 128, CHUNK), BF16),
            pltpu.VMEM((tokens, width), BF16),
            pltpu.VMEM((tokens, width), BF16),
            pltpu.VMEM((rows, feats), BF16),
            pltpu.VMEM((cols, 128), BF16),
            pltpu.VMEM((RANK, width), BF16),
            pltpu.VMEM((RANK, cols), BF16),
            pltpu.VMEM((cols, 2 * RANK), BF16),
            pltpu.VMEM((seqs, RANK, SEQ), F32),
            pltpu.VMEM((2, tokens, CHUNK), F32),
            pltpu.VMEM((tokens, 2 * RANK), F32),
            pltpu.VMEM((4, seqs, 8, 128), F32),
            pltpu.VMEM((4, seqs, 8, 128), F32),
            pltpu.VMEM((2, 4, 4, 64, 128), BF16),
            pltpu.VMEM((STRATA, PAD, feats), BF16),
            pltpu.VMEM((256, 256), BF16),
            pltpu.VMEM((4, rows // (2 * BLOCK), 16, BLOCK), BF16),
            pltpu.VMEM((4, rows // (2 * BLOCK), 16, BLOCK), BF16),
            pltpu.VMEM((4, rows // (2 * BLOCK), 16, BLOCK), BF16),
            pltpu.VMEM((evals, 1), I32),
            dma((6,)),
            dma((chunks,)),
            dma((2, 8)),
            dma((2, 8, chunks)),
            dma((2, 4)),
            dma((2, 2, chunks)),
            dma((3,)),
            dma((3,)),
            dma((16,)),
            dma((16,)),
            dma((2, 3)),
            dma((2, 3)),
            dma((2, 3)),
            dma((2, 3)),
            dma,
            dma,
        ],
        compiler_params=pltpu.CompilerParams(
            collective_id=0, has_side_effects=True, vmem_limit_bytes=57 * 2**20
        ),
    )(
        eval_inputs, eval_grads, w_gate, w_down, proj_in.T, proj_out.T, store_rows,
        eval_strata.reshape(1, evals), block_strata,
    )


def solution(mesh):
    return jax.shard_map(
        local,
        mesh=mesh,
        in_specs=(
            P("store", None),
            P("store", None),
            P("store", "tensor"),
            P("tensor", "store"),
            P(),
            P("tensor", None),
            P("store", "tensor"),
            P(),
            P("store"),
        ),
        out_specs=P("tensor", "store"),
        check_vma=False,
    )
```

time: 131 us -> 119 us (0.908)
  Pallas kernels: 124 us -> 117 us
  local copies, waits for them, and re-layouts: 6.35 us -> 2.06 us
    pallas_call x1, Pallas kernels: 124 us -> 117 us  [local(): pl.pallas_call(kernel, out_shape=jax.ShapeDtypeStruct((evals // 4, rows),...]
    unnamed x3 -> x1, local copies, waits for them, and re-layouts: 6.35 us -> 2.06 us
where the time goes in v2:
time: 119 us
  Pallas kernels  117 us (98%)
  local copies, waits for them, and re-layouts  2.06 us (2%)
    pallas_call x1, Pallas kernels, local(): pl.pallas_call(kernel, out_shape=jax.ShapeDtypeStruct((evals // 4, rows),...  117 us

profile of v2, /device:TPU:1, one launch (start us, length us, event | category | flops | bytes accessed | tf_op | source)
XLA Modules:
  0.0 119.0 jit_solution(5106008599365783936)
XLA Ops:
  0.0 116.9 %shard_map.91 = f32[48,4096]{1,0:T(8,128)} custom-call(bf16[768,4096]{1,0:T(8,128)(2,1)} %x_in.1, bf16[768,4096]{1,0:T(8,128)(2,1)} %g_in.1, bf16[128,1792]{1,0:T(8,128)(2,1)} %wg_in.1, bf16[1792,128]{1,0:T(8,128)(2,1)} %wd_in.1, bf16[64,4096]{1,0:T(8,128)(2,1)} %bitcast.3, bf16[64,1792]{1,0:T(8,128)(2,1)} %bitcast.4, bf16[4096,1024]{1,0:T(8,128)(2,1)} %st_in.1, ...), custom_call_target="tpu_custom_call" | custom-call | tf_op jit(solution)/shard_map/pallas_call | solution.py:419
  116.9 2.1 %copy.11 = f32[48,4096]{1,0:T(8,128)} copy(f32[48,4096]{1,0:T(8,128)} %shard_map.91) | data formatting | bytes 1572864

commit v3 on v2

--- a/solution.py
+++ b/solution.py
@@ -278,109 +278,8 @@
             device_id=(s, to), device_id_type=MESH,
         )
 
-    for i in range(3):
+    for i in (1, 0, 2):
         quarter(i, (t + i + 1) % 4, t).start()
-    total = pout[t]
-    for i in range(3):
-        quarter(i, (t + i + 1) % 4, (t + 3 - i) % 4).wait_recv()
-        total += rbuf[(t + 3 - i) % 4]
-    mine = (total * (1.0 / SEQ)).reshape(seqs * 8, 128).astype(BF16)
-    to, fr = iota((64, 48), 0), iota((64, 48), 1)
-    turn = jnp.logical_and(fr // 8 == to % 8, fr % 8 == to // 8).astype(F32).astype(BF16)
-    gat[c, z, x] = jnp.dot(turn, mine, preferred_element_type=F32).astype(BF16)
-
-    def flat_copy(i, zz, xx):
-        return pltpu.make_async_remote_copy(
-            src_ref=gat.at[c, zz, xx], dst_ref=gat.at[c, zz, xx], send_sem=psem.at[i], recv_sem=prem.at[i],
-            device_id=dev(z + i // 4, x + i % 4, c), device_id_type=MESH,
-        )
-
-    for i in (10, 6, 14, 9, 11, 2, 8, 5, 7, 13, 15, 1, 3, 4, 12):
-        flat_copy(i, z, x).start()
-
-    def flat_shared(ref):
-        return pltpu.make_async_remote_copy(
-            src_ref=ref, dst_ref=ref, send_sem=tsem, recv_sem=trem, device_id=sib, device_id_type=MESH
-        )
-
-    flat_shared(gat.at[c, z, x]).start()
-    for i in (1, 3, 4, 12, 5, 7, 13, 15, 2, 8, 6, 14, 9, 11, 10):
-        zz, xx = (z + 4 - i // 4) % 4, (x + 4 - i % 4) % 4
-        flat_copy(i, zz, xx).wait_recv()
-        flat_shared(gat.at[c, zz, xx]).start()
-    flat_shared(gat.at[1 - c]).wait_recv()
-    flats = gat[...].reshape(32, 64, 128).astype(F32)
-    for kk in range(8):
-        some = flats[:, kk * 8 : kk * 8 + 8, :].reshape(256, 128).astype(BF16)
-        rows = jnp.dot(place[...], some, preferred_element_type=F32).astype(BF16)
-        grouped[:, :, kk * 128 : (kk + 1) * 128] = rows.reshape(STRATA, PAD, 128)
-
-    def part_copy(g, i, to, at):
-        some = pl.ds(g * 8, 8)
-        return pltpu.make_async_remote_copy(
-            src_ref=part.at[to, some], dst_ref=got.at[at, some], send_sem=qsem.at[g, i], recv_sem=qrem.at[g, i],
-            device_id=(s, to), device_id_type=MESH,
-        )
-
-    def full_copy(g, i, to, at):
-        ref = full.at[at, pl.ds(g * 8, 8)]
-        return pltpu.make_async_remote_copy(
-            src_ref=ref, dst_ref=ref, send_sem=fsem.at[g, i], recv_sem=frem.at[g, i],
-            device_id=(s, to), device_id_type=MESH,
-        )
-
-    for g in range(2):
-
-        def blocks(p, _):
-            first = g * 8 + p * 4
-            found = []
-            for e in range(8):
-                b = 2 * first + e
-                stored = st[pl.ds(pl.multiple_of(b * BLOCK, BLOCK), BLOCK), :]
-                found.append(lax.dot_general(grouped[bs_ref[b]], stored, NT, preferred_element_type=F32))
-            for m in range(4):
-                for u in range(4):
-                    both = [r[u * 8 : u * 8 + 8] for r in found[2 * m : 2 * m + 2]]
-                    part[u, first + m] = jnp.concatenate(both, axis=0).astype(BF16)
-            return 0
-
-        lax.fori_loop(0, 2, blocks, 0)
-        for i in range(3):
-            part_copy(g, i, (t + i + 1) % 4, t).start()
-    for g in range(2):
-        for i in range(3):
-            part_copy(g, i, (t + i + 1) % 4, (t + 3 - i) % 4).wait_recv()
-        some = pl.ds(g * 8, 8)
-        total = part[t, some].astype(F32)
-        for i in range(3):
-            total += got[(t + 3 - i) % 4, some].astype(F32)
-        full[t, some] = total.astype(BF16)
-        for i in range(3):
-            full_copy(g, i, (t + i + 1) % 4, t).start()
-
-    own = slot[pl.ds(pl.multiple_of(t * 48, 8), 48), :]
-    entry = iota((96, 64), 1)
-    block_of = (entry // 8) % 2
-    rest_of = jnp.concatenate([own, own], axis=0) - (entry // 16) * 8 - entry % 8
-    rest_of = jnp.where(iota((96, 64), 0) // 48 == block_of, rest_of, -1)
-    for g in range(2):
-        for i in range(3):
-            full_copy(g, i, (t + i + 1) % 4, (t + 3 - i) % 4).wait_recv()
-
-        def expand(p, _):
-            for e in range(4):
-                m = g * 8 + p * 4 + e
-                chosen = rest_of == jnp.where(block_of == 0, bs_ref[2 * m] * PAD, bs_ref[2 * m + 1] * PAD)
-                summed = jnp.dot(
-                    chosen.astype(F32).astype(BF16), full[:, m].reshape(64, 128), preferred_element_type=F32
-                )
-                at = pl.multiple_of(m * 2 * BLOCK, 2 * BLOCK)
-                out[:, pl.ds(at, BLOCK)] = summed[0:48]
-                out[:, pl.ds(at + BLOCK, BLOCK)] = summed[48:96]
-            return 0
-
-        lax.fori_loop(0, 2, expand, 0)
-
     for ty in range(2):
         buf, a, b, bm, bp, am, ap = sides(ty)
         own_buf = buf.at[:, c]
@@ -396,6 +295,67 @@
                 src_ref=ref, dst_ref=ref, send_sem=sibs.at[ty, i], recv_sem=sibr.at[ty, 0, 0],
                 device_id=sib, device_id_type=MESH,
             ).wait_send()
+    total = pout[t]
+    for i in range(3):
+        quarter(i, (t + i + 1) % 4, (t + 3 - i) % 4).wait_recv()
+        total += rbuf[(t + 3 - i) % 4]
+    mine = (total * (1.0 / SEQ)).reshape(seqs * 8, 128).astype(BF16)
+    to, fr = iota((64, 48), 0), iota((64, 48), 1)
+    turn = jnp.logical_and(fr // 8 == to % 8, fr % 8 == to // 8).astype(F32).astype(BF16)
+    gat[c, z, x] = jnp.dot(turn, mine, preferred_element_type=F32).astype(BF16)
+
+    def flat_copy(i, zz, xx):
+        return pltpu.make_async_remote_copy(
+            src_ref=gat.at[c, zz, xx], dst_ref=gat.at[c, zz, xx], send_sem=psem.at[i], recv_sem=prem.at[i],
+            device_id=dev(z + i // 4, x + i % 4, c), device_id_type=MESH,
+        )
+
+    for i in (10, 6, 14, 9, 11, 2, 8, 5, 7, 13, 15, 1, 3, 4, 12):
+        flat_copy(i, z, x).start()
+
+    def flat_shared(ref):
+        return pltpu.make_async_remote_copy(
+            src_ref=ref, dst_ref=ref, send_sem=tsem, recv_sem=trem, device_id=sib, device_id_type=MESH
+        )
+
+    flat_shared(gat.at[c, z, x]).start()
+    for i in (1, 3, 4, 12, 5, 7, 13, 15, 2, 8, 6, 14, 9, 11, 10):
+        zz, xx = (z + 4 - i // 4) % 4, (x + 4 - i % 4) % 4
+        flat_copy(i, zz, xx).wait_recv()
+        flat_shared(gat.at[c, zz, xx]).start()
+    flat_shared(gat.at[1 - c]).wait_recv()
+    flats = gat[...].reshape(32, 64, 128).astype(F32)
+    lines = [flats[:, kk * 8 : kk * 8 + 8, :].reshape(256, 128).astype(BF16) for kk in range(8)]
+    placed = jnp.dot(place[...], jnp.concatenate(lines, axis=1), preferred_element_type=F32)
+    grouped[...] = placed.astype(BF16).reshape(grouped.shape)
+
+    def part_copy(g, i, to, at):
+        some = pl.ds(g * 8, 8)
+        return pltpu.make_async_remote_copy(
+            src_ref=part.at[to, some], dst_ref=got.at[at, some], send_sem=qsem.at[g, i], recv_sem=qrem.at[g, i],
+            device_id=(s, to), device_id_type=MESH,
+        )
+
+    def full_copy(g, i, to, at):
+        ref = full.at[at, pl.ds(g * 8, 8)]
+        return pltpu.make_async_remote_copy(
+            src_ref=ref, dst_ref=ref, send_sem=fsem.at[g, i], recv_sem=frem.at[g, i],
+            device_id=(s, to), device_id_type=MESH,
+        )
+
+    for g in range(2):
+
+        first = g * 8
+        found = []
+        for b in range(2 * first, 2 * first + 16):
+            stored = st[b * BLOCK : (b + 1) * BLOCK, :]
+            found.append(lax.dot_general(grouped[bs_ref[b]], stored, NT, preferred_element_type=F32))
+        for m in range(8):
+            for u in range(4):
+                both = [r[u * 8 : u * 8 + 8] for r in found[2 * m : 2 * m + 2]]
+                part[u, first + m] = jnp.concatenate(both, axis=0).astype(BF16)
+        for i in (1, 0, 2):
+            part_copy(g, i, (t + i + 1) % 4, t).start()
     for i in range(3):
         quarter(i, (t + i + 1) % 4, t).wait_send()
     for i in range(1, 16):
@@ -403,7 +363,42 @@
     flat_shared(gat.at[c]).wait_send()
     for g in range(2):
         for i in range(3):
+            part_copy(g, i, (t + i + 1) % 4, (t + 3 - i) % 4).wait_recv()
+        some = pl.ds(g * 8, 8)
+        total = part[t, some].astype(F32)
+        for i in range(3):
+            total += got[(t + 3 - i) % 4, some].astype(F32)
+        full[t, some] = total.astype(BF16)
+        for i in (1, 0, 2):
+            full_copy(g, i, (t + i + 1) % 4, t).start()
+    for g in range(2):
+        for i in range(3):
             part_copy(g, i, (t + i + 1) % 4, t).wait_send()
+
+    own = slot[pl.ds(pl.multiple_of(t * 48, 8), 48), :]
+    entry = iota((96, 64), 1)
+    block_of = (entry // 8) % 2
+    rest_of = jnp.concatenate([own, own], axis=0) - (entry // 16) * 8 - entry % 8
+    rest_of = jnp.where(iota((96, 64), 0) // 48 == block_of, rest_of, -1)
+    for g in range(2):
+        for i in range(3):
+            full_copy(g, i, (t + i + 1) % 4, (t + 3 - i) % 4).wait_recv()
+
+        def expand(p, _):
+            for e in range(4):
+                m = g * 8 + p * 4 + e
+                chosen = rest_of == jnp.where(block_of == 0, bs_ref[2 * m] * PAD, bs_ref[2 * m + 1] * PAD)
+                summed = jnp.dot(
+                    chosen.astype(F32).astype(BF16), full[:, m].reshape(64, 128), preferred_element_type=F32
+                )
+                at = pl.multiple_of(m * 2 * BLOCK, 2 * BLOCK)
+                out[:, pl.ds(at, BLOCK)] = summed[0:48]
+                out[:, pl.ds(at + BLOCK, BLOCK)] = summed[48:96]
+            return 0
+
+        lax.fori_loop(0, 2, expand, 0)
+    for g in range(2):
+        for i in range(3):
             full_copy(g, i, (t + i + 1) % 4, t).wait_send()
 
 

time: 119 us -> 118 us (level)
  no operation moved by 1% of the time
where the time goes in v3:
time: 118 us
  Pallas kernels  116 us (98%)
  local copies, waits for them, and re-layouts  2.06 us (2%)
    pallas_call x1, Pallas kernels, local(): pl.pallas_call(kernel, out_shape=jax.ShapeDtypeStruct((evals // 4, rows),...  116 us

profile of v3, /device:TPU:1, one launch (start us, length us, event | category | flops | bytes accessed | tf_op | source)
XLA Modules:
  0.0 118.0 jit_solution(3420806224425553085)
XLA Ops:
  0.0 115.9 %shard_map.91 = f32[48,4096]{1,0:T(8,128)} custom-call(bf16[768,4096]{1,0:T(8,128)(2,1)} %x_in.1, bf16[768,4096]{1,0:T(8,128)(2,1)} %g_in.1, bf16[128,1792]{1,0:T(8,128)(2,1)} %wg_in.1, bf16[1792,128]{1,0:T(8,128)(2,1)} %wd_in.1, bf16[64,4096]{1,0:T(8,128)(2,1)} %bitcast.3, bf16[64,1792]{1,0:T(8,128)(2,1)} %bitcast.4, bf16[4096,1024]{1,0:T(8,128)(2,1)} %st_in.1, ...), custom_call_target="tpu_custom_call" | custom-call | tf_op jit(solution)/shard_map/pallas_call | solution.py:414
  115.9 2.1 %copy.11 = f32[48,4096]{1,0:T(8,128)} copy(f32[48,4096]{1,0:T(8,128)} %shard_map.91) | data formatting | bytes 1572864

commit v4 on v3

--- a/solution.py
+++ b/solution.py
@@ -11,9 +11,8 @@
 RANK, SEQ, BLOCK, STRATA = 64, 128, 128, 8
 PAD = 32
 CHUNK = 256
-AHEAD1, AHEAD2, AHEAD3 = 6, 4, 2
-ORDER = "edrabRcmM"
-TILE = 384
+AHEAD1, AHEAD2, AHEAD3 = 8, 4, 2
+ORDER = "edabcrm"
 BF16, F32, I32 = jnp.bfloat16, jnp.float32, jnp.int32
 HIGH = lax.Precision.HIGHEST
 NT = (((1,), (1,)), ((), ()))
@@ -182,25 +181,23 @@
                 total = term if total is None else total + term
         return total
 
-    def most(j, part):
+    def most(j):
         @within(j)
         def _():
-            at = pl.ds(part * TILE, TILE)
-            for ty in range(2):
-                if part == 0:
-                    from_sibling(ty, j, 0).wait_recv()
+            at = slice(None)
+            for ty in range(2):
+                from_sibling(ty, j, 0).wait_recv()
             for ty in range(2):
                 a = (z, x)[ty]
                 acc[ty, at, :] = product(at, ty, j, [a, (a + 1) % 4, (a + 3) % 4])
 
-    def rest(j, part):
+    def rest(j):
         @within(j - 1)
         def _():
             k = j - 1
-            at = pl.ds(part * TILE, TILE)
-            for ty in range(2):
-                if part == 0:
-                    from_sibling(ty, k, 1).wait_recv()
+            at = slice(None)
+            for ty in range(2):
+                from_sibling(ty, k, 1).wait_recv()
             proj = po2[pl.ds(pl.multiple_of(k * CHUNK, CHUNK), CHUNK), :]
             gate = acc[0, at, :] + product(at, 0, k, [(z + 2) % 4])
             back = acc[1, at, :] + product(at, 1, k, [(x + 2) % 4])
@@ -238,12 +235,12 @@
         lt[m] = lax.dot_general(pin[...], xv[m * SEQ : (m + 1) * SEQ, :], NT, preferred_element_type=F32)
 
     work = {
-        0: [loads],
-        1: [tables],
-        2: [projections],
+        2: [loads],
+        3: [tables],
+        4: [projections],
     }
     for m in range(seqs):
-        work.setdefault(3 + m // 2, []).append(functools.partial(lefts, m))
+        work.setdefault(5 + m // 2, []).append(functools.partial(lefts, m))
     for j in range(AHEAD1):
         for f in (first_hop, second_hop, third_hop):
             f(j - AHEAD1)
@@ -254,8 +251,7 @@
 
     steps = {
         "a": first_hop, "b": second_hop, "c": third_hop, "d": fourth_hop, "e": last_line,
-        "m": functools.partial(most, part=0), "M": functools.partial(most, part=1),
-        "r": functools.partial(rest, part=0), "R": functools.partial(rest, part=1),
+        "m": most, "r": rest,
     }
 
     def steady(j, _):

time: 118 us -> 117 us (level)
  Pallas kernels: 116 us -> 114 us
    pallas_call x1, Pallas kernels: 116 us -> 114 us  [local(): pl.pallas_call(kernel, out_shape=jax.ShapeDtypeStruct((evals // 4, rows),...]
where the time goes in v4:
time: 117 us; the launch traced here: 116 us
  Pallas kernels  114 us (97%)
  local copies, waits for them, and re-layouts  2.06 us (2%)
    pallas_call x1, Pallas kernels, local(): pl.pallas_call(kernel, out_shape=jax.ShapeDtypeStruct((evals // 4, rows),...  114 us

profile of v4, /device:TPU:1, one launch (start us, length us, event | category | flops | bytes accessed | tf_op | source)
XLA Modules:
  0.0 116.5 jit_solution(7543964035007142129)
XLA Ops:
  0.0 114.4 %shard_map.91 = f32[48,4096]{1,0:T(8,128)} custom-call(bf16[768,4096]{1,0:T(8,128)(2,1)} %x_in.1, bf16[768,4096]{1,0:T(8,128)(2,1)} %g_in.1, bf16[128,1792]{1,0:T(8,128)(2,1)} %wg_in.1, bf16[1792,128]{1,0:T(8,128)(2,1)} %wd_in.1, bf16[64,4096]{1,0:T(8,128)(2,1)} %bitcast.3, bf16[64,1792]{1,0:T(8,128)(2,1)} %bitcast.4, bf16[4096,1024]{1,0:T(8,128)(2,1)} %st_in.1, ...), custom_call_target="tpu_custom_call" | custom-call | tf_op jit(solution)/shard_map/pallas_call | solution.py:410
  114.4 2.1 %copy.11 = f32[48,4096]{1,0:T(8,128)} copy(f32[48,4096]{1,0:T(8,128)} %shard_map.91) | data formatting | bytes 1572864

commit v5 on v4

--- a/solution.py
+++ b/solution.py
@@ -12,7 +12,7 @@
 PAD = 32
 CHUNK = 256
 AHEAD1, AHEAD2, AHEAD3 = 8, 4, 2
-ORDER = "edabcrm"
+ORDER = "derabcm"
 BF16, F32, I32 = jnp.bfloat16, jnp.float32, jnp.int32
 HIGH = lax.Precision.HIGHEST
 NT = (((1,), (1,)), ((), ()))

time: 117 us -> 116 us (level)
  no operation moved by 1% of the time
where the time goes in v5:
time: 116 us
  Pallas kernels  114 us (98%)
  local copies, waits for them, and re-layouts  2.06 us (2%)
    pallas_call x1, Pallas kernels, local(): pl.pallas_call(kernel, out_shape=jax.ShapeDtypeStruct((evals // 4, rows),...  114 us

profile of v5, /device:TPU:1, one launch (start us, length us, event | category | flops | bytes accessed | tf_op | source)
XLA Modules:
  0.0 116.1 jit_solution(10106310598674827981)
XLA Ops:
  0.0 114.0 %shard_map.91 = f32[48,4096]{1,0:T(8,128)} custom-call(bf16[768,4096]{1,0:T(8,128)(2,1)} %x_in.1, bf16[768,4096]{1,0:T(8,128)(2,1)} %g_in.1, bf16[128,1792]{1,0:T(8,128)(2,1)} %wg_in.1, bf16[1792,128]{1,0:T(8,128)(2,1)} %wd_in.1, bf16[64,4096]{1,0:T(8,128)(2,1)} %bitcast.3, bf16[64,1792]{1,0:T(8,128)(2,1)} %bitcast.4, bf16[4096,1024]{1,0:T(8,128)(2,1)} %st_in.1, ...), custom_call_target="tpu_custom_call" | custom-call | tf_op jit(solution)/shard_map/pallas_call | solution.py:410
  114.0 2.1 %copy.11 = f32[48,4096]{1,0:T(8,128)} copy(f32[48,4096]{1,0:T(8,128)} %shard_map.91) | data formatting | bytes 1572864
